TPU v7x, 32 devices: a whole 2x2x4 slice. The times are simulated.
32 devices in a mesh: groups: 2 (over y), rows: 4 (over z), cols: 2 (over x), sub: 2 (over core).
Axes of the slice: x: 2, y: 2, z: 4, core: 2. Of those that a mesh axis runs over, the one named last changes fastest.
Arguments:
- data_rows: bfloat16 [16384, 256], P(('groups', 'rows')), parts along dimension 0, may hold values from -6 to 6
- landmarks: bfloat16 [4096, 256], P(('groups', 'rows', 'cols')), parts along dimension 0, may hold values from -6 to 6
- factor: bfloat16 [4096, 2048], P(('groups', 'rows', 'cols'), 'sub'), parts along dimension 0, may hold values from -0.02734375 to 0.02734375
- chosen_owner: int32 [2048, 1], P('groups'), parts along dimension 0, may hold values from 0 to 3; in each aligned block of 256 rows (0 to 255, 256 to 511, ...) at most 256 rows name the same one
- chosen_local: int32 [2048], P('groups'), parts along dimension 0, may hold values from 0 to 2047
Outputs:
- leverage: float32 [16384], P(('groups', 'rows', 'cols')), parts along dimension 0
- panel: float32 [2048, 256], P(('groups', 'rows'), 'cols'), parts along dimension 0
There are 2 independent parts, one for each index of `groups`. A program takes and returns all parts, laid end to end along the dimension named above; each array names one. Nothing has to cross between parts.
Inputs may be any that keep to these rules, and one draw needn't show every extreme that they name: `chosen_owner`: in each aligned block of 256 chosen rows no owner appears more than 256 times, and in some block one owner appears exactly 256 times.
All inputs are finite; a program needn't handle non-finite values.
Results may differ from a plain program's by a relative error of at most 0.00039.
Values may be sent and summed in bfloat16 or wider, within the bound.
A program may use at most 64 MiB of HBM per device.

v0:
```python
import math

import jax
import jax.numpy as jnp
from jax import lax
from jax.sharding import PartitionSpec as P

PANEL_DEV = 64


def squared_norms(rows_in):
    return jnp.sum(jnp.square(rows_in.astype(jnp.float32)), axis=1)


def kernel_values(left, right, right_sq, rate_value, depth):
    left_sq = squared_norms(left)
    cross = lax.dot_general(
        left, right, (((1,), (1,)), ((), ())), preferred_element_type=jnp.float32
    )
    distance = left_sq[:, None] + right_sq[None, :] - 2.0 * cross
    return jnp.exp(rate_value * (2.0 * depth - distance))


def shards(data_rows, landmarks, factor, chosen_owner, chosen_local):
    slab_rows, depth = data_rows.shape
    rate_value = 0.3 / math.sqrt(8.0 * depth)
    amplitude = math.exp(2.0 * rate_value * depth)
    col_count = lax.axis_size("cols")
    sub_count = lax.axis_size("sub")
    row_count = lax.axis_size("rows")
    col_index = lax.axis_index("cols")
    sub_index = lax.axis_index("sub")
    row_index = lax.axis_index("rows")
    every_land = lax.all_gather(landmarks, ("rows", "cols"), axis=0, tiled=True)
    mixed = lax.all_to_all(factor, "cols", split_axis=1, concat_axis=0, tiled=True)
    factor_cols = lax.all_gather(mixed, "rows", axis=0, tiled=True)
    land_sq = squared_norms(every_land)
    block_rows = math.gcd(slab_rows, 256)
    blocks = data_rows.reshape(-1, block_rows, depth)

    def block_total(block):
        values = kernel_values(block, every_land, land_sq, rate_value, depth).astype(jnp.bfloat16)
        projected = jnp.dot(values, factor_cols, preferred_element_type=jnp.float32)
        return jnp.sum(projected * projected, axis=1)

    totals = lax.map(block_total, blocks).reshape(-1)
    row_totals = lax.psum_scatter(totals, "cols", scatter_dimension=0, tiled=True)
    approx = lax.psum(row_totals, "sub")
    leverage = (amplitude - approx) / 8.0
    block_owners = chosen_owner[:, 0].reshape(row_count, -1)
    local_rows = chosen_local.reshape(row_count, -1)
    chosen_dev = block_owners.shape[1]
    capacity = 8 * max(1, chosen_dev // (2 * row_count))
    mine_mask = (block_owners == row_index).astype(jnp.int32)
    slot_rank = jnp.cumsum(mine_mask, axis=1) - mine_mask
    replicas = col_count * sub_count
    share_size = capacity // replicas
    replica_index = col_index * sub_count + sub_index
    slot_ids = replica_index * share_size + jnp.arange(share_size, dtype=jnp.int32)
    picked = (mine_mask[:, None, :] == 1) & (slot_rank[:, None, :] == slot_ids[None, :, None])
    source = jnp.sum(jnp.where(picked, local_rows[:, None, :], 0), axis=2)
    filled = jnp.any(picked, axis=2)
    picked_rows = jnp.take(data_rows, source.reshape(-1), axis=0).reshape(
        row_count, share_size, depth
    )
    outgoing = jnp.where(filled[:, :, None], picked_rows, jnp.zeros((), jnp.bfloat16))
    moved = lax.all_to_all(outgoing, "rows", split_axis=0, concat_axis=0, tiled=True)
    arrived = lax.all_gather(moved, ("cols", "sub"), axis=1, tiled=True)
    block_owner = lax.dynamic_index_in_dim(block_owners, row_index, 0, keepdims=False)
    before = jnp.tril(jnp.ones((chosen_dev, chosen_dev), jnp.bool_), -1)
    matched = (block_owner[:, None] == block_owner[None, :]) & before
    own_rank = jnp.sum(matched.astype(jnp.int32), axis=1)
    flattened = arrived.reshape(row_count * capacity, depth)
    chosen_rows = jnp.take(flattened, block_owner * capacity + own_rank, axis=0)
    per_block = PANEL_DEV // col_count
    piece = lax.dynamic_slice_in_dim(chosen_rows, col_index * per_block, per_block, 0)
    column_rows = lax.all_gather(piece, "rows", axis=0, tiled=True)
    panel = kernel_values(chosen_rows, column_rows, squared_norms(column_rows), rate_value, depth)
    return (leverage, panel)


def solution(mesh):
    placed = (
        P(("groups", "rows"), None),
        P(("groups", "rows", "cols"), None),
        P(("groups", "rows", "cols"), "sub"),
        P("groups", None),
        P("groups"),
    )
    return jax.shard_map(
        shards,
        mesh=mesh,
        in_specs=placed,
        out_specs=(P(("groups", "rows", "cols")), P(("groups", "rows"), "cols")),
        check_vma=False,
    )
```

profile of v0, /device:TPU:0, one launch (start us, length us, event | category | flops | bytes accessed | tf_op | source)
XLA Modules:
  0.0 143.4 jit_solution(4056909570043862323)
XLA Ops:
  7.2 0.0 copy-start.2
  7.2 0.0 copy-start.3
  7.2 0.0 copy-start
  7.2 0.0 all-gather.3.cloned.1.call-start
  7.2 0.7 all-gather.3.cloned.1.call-update
  7.9 0.0 copy-start.4
  7.9 1.9 %copy.21 = bf16[32,2,8,512]{3,2,0,1:T(8,128)(2,1)} copy(bf16[32,2,8,512]{3,2,1,0:T(8,128)(2,1)} %bitcast.51) | data formatting | bytes 1048576 | tf_op jit(solution)/shard_map/all_to_all | solution.py:35
  9.8 4.2 %all-to-all-start = ((bf16[256,2,512]{2,0,1:T(8,128)(2,1)}), bf16[256,2,512]{2,0,1:T(8,128)(2,1)S(1)}, u32[]{:S(2)}, u32[]{:S(2)}) async-start(bf16[256,2,512]{2,0,1:T(8,128)(2,1)} %bitcast.37), calls=%async_computation | async-start | bytes 1048576 | tf_op jit(solution)/shard_map/all_to_all | solution.py:35
  14.0 0.0 all-gather.5.cloned.1.call-start
  14.1 0.5 broadcast.128
  14.6 0.0 copy-done.2
  14.6 0.7 reduce.3
  15.3 1.2 reduce-window.6
  16.5 0.1 slice.12
  16.6 0.1 copy.14
  16.7 0.1 copy.15
  16.8 0.1 add_bitcast_fusion
  16.9 5.9 %all-to-all-done = bf16[256,2,512]{2,0,1:T(8,128)(2,1)S(1)} async-done(((bf16[256,2,512]{2,0,1:T(8,128)(2,1)}), bf16[256,2,512]{2,0,1:T(8,128)(2,1)S(1)}, u32[]{:S(2)}, u32[]{:S(2)}) %all-to-all-start) | async-done | bytes 524320 | tf_op jit(solution)/shard_map/all_to_all | solution.py:35
  22.8 0.0 copy-start.1
  22.8 0.8 copy-done.1
  23.6 0.0 all-gather.5.cloned.1.call-update
  23.6 0.0 copy-done.3
  23.6 0.2 select_reduce_fusion
  23.9 0.1 reshape.144
  24.0 0.0 copy-done
  24.0 1.2 gather_fusion
  25.1 0.2 fusion.20
  25.4 0.8 select_select_fusion
  26.2 5.1 %all-to-all-start.1 = ((bf16[4,64,256]{2,1,0:T(8,128)(2,1)}), bf16[4,64,256]{2,1,0:T(8,128)(2,1)S(1)}, u32[]{:S(2)}, u32[]{:S(2)}) async-start(bf16[4,64,256]{2,1,0:T(8,128)(2,1)} %select_select_fusion), calls=%async_computation.1 | async-start | bytes 262144 | tf_op jit(solution)/shard_map/all_to_all | solution.py:67
  31.3 0.0 copy-done.4
  31.3 0.6 dynamic-slice
  32.5 0.2 convert_reduce_fusion
  32.7 4.5 %all-to-all-done.1 = bf16[4,64,256]{2,1,0:T(8,128)(2,1)S(1)} async-done(((bf16[4,64,256]{2,1,0:T(8,128)(2,1)}), bf16[4,64,256]{2,1,0:T(8,128)(2,1)S(1)}, u32[]{:S(2)}, u32[]{:S(2)}) %all-to-all-start.1) | async-done | bytes 131104 | tf_op jit(solution)/shard_map/all_to_all | solution.py:67
  37.2 9.6 %all_gather.14 = bf16[4,256,256]{2,1,0:T(8,128)(2,1)S(1)} all-gather(bf16[4,64,256]{2,1,0:T(8,128)(2,1)S(1)} %all-to-all-done.1), channel_id=1, replica_groups=mesh['groups'=2,'rows'=4,'cols'=2,'sub'=2] {'cols','sub'}, dimensions={1}, use_global_device_ids=true | all-gather | bytes 655360 | tf_op jit(solution)/shard_map/all_gather | solution.py:68
  46.8 1.1 gather_fusion.1
  48.0 0.2 multiply_reduce_fusion.2
  48.2 13.2 %all_gather.15 = bf16[128,256]{1,0:T(8,128)(2,1)S(1)} all-gather(bf16[32,256]{1,0:T(8,128)(2,1)S(1)} %constant_dynamic-slice_fusion), channel_id=1, replica_groups=mesh['groups'=2,'rows'=4,'cols'=2,'sub'=2] {'rows'}, dimensions={0}, use_global_device_ids=true | all-gather | bytes 81920 | tf_op jit(solution)/shard_map/all_gather | solution.py:77
  61.4 0.1 multiply_reduce_fusion.3
  61.5 0.9 fusion.18
  62.4 0.0 all-gather.3.cloned.1.call-done
  62.4 1.6 %multiply_reduce_fusion.1 = f32[2048]{0:T(1024)S(1)} fusion(bf16[2048,256]{1,0:T(8,128)(2,1)} %all-gather.3.cloned.1.call-done), kind=kLoop, calls=%fused_computation.17 | loop fusion | flops 1570816 | bytes 1056768 | tf_op jit(solution)/shard_map/reduce_sum | solution.py:12
  64.0 36.9 %all-gather.5.cloned.1.call-done = bf16[2048,512]{1,0:T(8,128)(2,1)} async-done(((bf16[512,512]{1,0:T(8,128)(2,1)}), bf16[2048,512]{1,0:T(8,128)(2,1)}) %all-gather.5.cloned.1.call-update) | async-done | bytes 2097168 | tf_op jit(solution)/shard_map/all_gather | solution.py:36
  100.9 27.6 %while.10 = (s32[]{:T(128)}, f32[8,256]{1,0:T(8,128)S(1)}, bf16[8,256,256]{2,1,0:T(8,128)(2,1)S(1)}, f32[2048]{0:T(1024)S(1)}, bf16[2048,256]{1,0:T(8,128)(2,1)}...) while((s32[]{:T(128)}, f32[8,256]{1,0:T(8,128)S(1)}, bf16[8,256,256]{2,1,0:T(8,128)(2,1)S(1)}, ...), condition=%wide.region_4.5_spmd, body=%wide.region_1.4_spmd.sunk | while | flops 808910336 | bytes 3421289 | solution.py:46
  100.9 0.1 multiply_reduce_fusion.5
  101.0 3.3 %fusion.32 = f32[256]{0:T(256)S(1)} fusion(bf16[2048,512]{1,0:T(8,128)(2,1)} %get-tuple-element.109, bf16[2048,256]{1,0:T(8,128)(2,1)} %get-tuple-element.108, f32[2048]{0:T(1024)S(1)} %get-tuple-element.107, f32[256]{0:T(256)S(1)} %multiply_reduce_fusion.5, bf16[8,256,256]{2,1,0:T(8,128)(2,1)S(1)} %get-tuple-element.106, s32[]{:T(128)S(6)} %copy.25), kind=kOutput, calls=%fused_computation.9.clone.1 | convolution fusion | flops 808713984 | bytes 3287044 | tf_op jit(solution)/shard_map/while/body/eval_jaxpr/dot_general | solution.py:43
  104.3 0.1 multiply_reduce_fusion.5
  104.5 3.3 %fusion.32 = f32[256]{0:T(256)S(1)} fusion(bf16[2048,512]{1,0:T(8,128)(2,1)} %get-tuple-element.109, bf16[2048,256]{1,0:T(8,128)(2,1)} %get-tuple-element.108, f32[2048]{0:T(1024)S(1)} %get-tuple-element.107, f32[256]{0:T(256)S(1)} %multiply_reduce_fusion.5, bf16[8,256,256]{2,1,0:T(8,128)(2,1)S(1)} %get-tuple-element.106, s32[]{:T(128)S(6)} %copy.25), kind=kOutput, calls=%fused_computation.9.clone.1 | convolution fusion | flops 808713984 | bytes 3287044 | tf_op jit(solution)/shard_map/while/body/eval_jaxpr/dot_general | solution.py:43
  107.8 0.1 multiply_reduce_fusion.5
  107.9 3.3 %fusion.32 = f32[256]{0:T(256)S(1)} fusion(bf16[2048,512]{1,0:T(8,128)(2,1)} %get-tuple-element.109, bf16[2048,256]{1,0:T(8,128)(2,1)} %get-tuple-element.108, f32[2048]{0:T(1024)S(1)} %get-tuple-element.107, f32[256]{0:T(256)S(1)} %multiply_reduce_fusion.5, bf16[8,256,256]{2,1,0:T(8,128)(2,1)S(1)} %get-tuple-element.106, s32[]{:T(128)S(6)} %copy.25), kind=kOutput, calls=%fused_computation.9.clone.1 | convolution fusion | flops 808713984 | bytes 3287044 | tf_op jit(solution)/shard_map/while/body/eval_jaxpr/dot_general | solution.py:43
  111.2 0.1 multiply_reduce_fusion.5
  111.4 3.3 %fusion.32 = f32[256]{0:T(256)S(1)} fusion(bf16[2048,512]{1,0:T(8,128)(2,1)} %get-tuple-element.109, bf16[2048,256]{1,0:T(8,128)(2,1)} %get-tuple-element.108, f32[2048]{0:T(1024)S(1)} %get-tuple-element.107, f32[256]{0:T(256)S(1)} %multiply_reduce_fusion.5, bf16[8,256,256]{2,1,0:T(8,128)(2,1)S(1)} %get-tuple-element.106, s32[]{:T(128)S(6)} %copy.25), kind=kOutput, calls=%fused_computation.9.clone.1 | convolution fusion | flops 808713984 | bytes 3287044 | tf_op jit(solution)/shard_map/while/body/eval_jaxpr/dot_general | solution.py:43
  114.7 0.1 multiply_reduce_fusion.5
  114.8 3.3 %fusion.32 = f32[256]{0:T(256)S(1)} fusion(bf16[2048,512]{1,0:T(8,128)(2,1)} %get-tuple-element.109, bf16[2048,256]{1,0:T(8,128)(2,1)} %get-tuple-element.108, f32[2048]{0:T(1024)S(1)} %get-tuple-element.107, f32[256]{0:T(256)S(1)} %multiply_reduce_fusion.5, bf16[8,256,256]{2,1,0:T(8,128)(2,1)S(1)} %get-tuple-element.106, s32[]{:T(128)S(6)} %copy.25), kind=kOutput, calls=%fused_computation.9.clone.1 | convolution fusion | flops 808713984 | bytes 3287044 | tf_op jit(solution)/shard_map/while/body/eval_jaxpr/dot_general | solution.py:43
  118.2 0.1 multiply_reduce_fusion.5
  118.3 3.3 %fusion.32 = f32[256]{0:T(256)S(1)} fusion(bf16[2048,512]{1,0:T(8,128)(2,1)} %get-tuple-element.109, bf16[2048,256]{1,0:T(8,128)(2,1)} %get-tuple-element.108, f32[2048]{0:T(1024)S(1)} %get-tuple-element.107, f32[256]{0:T(256)S(1)} %multiply_reduce_fusion.5, bf16[8,256,256]{2,1,0:T(8,128)(2,1)S(1)} %get-tuple-element.106, s32[]{:T(128)S(6)} %copy.25), kind=kOutput, calls=%fused_computation.9.clone.1 | convolution fusion | flops 808713984 | bytes 3287044 | tf_op jit(solution)/shard_map/while/body/eval_jaxpr/dot_general | solution.py:43
  121.6 0.1 multiply_reduce_fusion.5
  121.7 3.3 %fusion.32 = f32[256]{0:T(256)S(1)} fusion(bf16[2048,512]{1,0:T(8,128)(2,1)} %get-tuple-element.109, bf16[2048,256]{1,0:T(8,128)(2,1)} %get-tuple-element.108, f32[2048]{0:T(1024)S(1)} %get-tuple-element.107, f32[256]{0:T(256)S(1)} %multiply_reduce_fusion.5, bf16[8,256,256]{2,1,0:T(8,128)(2,1)S(1)} %get-tuple-element.106, s32[]{:T(128)S(6)} %copy.25), kind=kOutput, calls=%fused_computation.9.clone.1 | convolution fusion | flops 808713984 | bytes 3287044 | tf_op jit(solution)/shard_map/while/body/eval_jaxpr/dot_general | solution.py:43
  125.1 0.1 multiply_reduce_fusion.5
  125.2 3.3 %fusion.32 = f32[256]{0:T(256)S(1)} fusion(bf16[2048,512]{1,0:T(8,128)(2,1)} %get-tuple-element.109, bf16[2048,256]{1,0:T(8,128)(2,1)} %get-tuple-element.108, f32[2048]{0:T(1024)S(1)} %get-tuple-element.107, f32[256]{0:T(256)S(1)} %multiply_reduce_fusion.5, bf16[8,256,256]{2,1,0:T(8,128)(2,1)S(1)} %get-tuple-element.106, s32[]{:T(128)S(6)} %copy.25), kind=kOutput, calls=%fused_computation.9.clone.1 | convolution fusion | flops 808713984 | bytes 3287044 | tf_op jit(solution)/shard_map/while/body/eval_jaxpr/dot_general | solution.py:43
  128.5 5.0 %all-reduce = f32[2048]{0:T(1024)S(1)} all-reduce(f32[2048]{0:T(1024)S(1)} %bitcast.53), channel_id=2, replica_groups=mesh['groups'=2,'rows'=4,'cols'=2,'sub'=2] {'cols'}, use_global_device_ids=true, to_apply=%region_5.6.clone | all-reduce | flops 2048 | bytes 16384
  133.5 2.5 %psum.7 = f32[1024]{0:T(1024)S(1)} all-reduce(f32[1024]{0:T(1024)S(1)} %dynamic-slice.1), channel_id=1, replica_groups=mesh['groups'=2,'rows'=4,'cols'=2,'sub'=2] {'sub'}, use_global_device_ids=true, to_apply=%region_6.7 | all-reduce | flops 1024 | bytes 8192 | tf_op jit(solution)/shard_map/psum | solution.py:48
  136.0 0.6 subtract_multiply_fusion
  (28 shorter events, 0.5 us)
Async XLA Ops:
  7.2 7.4 %copy-start.2 = (s32[1024,1]{0,1:T(1,128)S(1)}, s32[1024,1]{0,1:T(1,128)}, u32[]{:S(2)}) copy-start(s32[1024,1]{0,1:T(1,128)} %param.10) | copy-start | bytes 12292
  7.2 16.4 %copy-start.3 = (s32[1024]{0:T(1024)S(1)}, s32[1024]{0:T(1024)}, u32[]{:S(2)}) copy-start(s32[1024]{0:T(1024)} %param.11) | copy-start | bytes 12292
  7.2 16.8 %copy-start = (bf16[2048,256]{1,0:T(8,128)(2,1)S(1)}, bf16[2048,256]{1,0:T(8,128)(2,1)}, u32[]{:S(2)}) copy-start(bf16[2048,256]{1,0:T(8,128)(2,1)} %param.7) | copy-start | bytes 3145732
  7.2 55.2 %all-gather.3.cloned.1.call-start = ((), (), s32[]{:S(2)}) async-start(), calls=%async_computation.2 | async-start | bytes 1179648 | tf_op jit(solution)/shard_map/all_gather | solution.py:34
  7.9 23.4 %copy-start.4 = (u32[32]{0:T(128)S(1)}, u32[32]{0:T(128)}, u32[]{:S(2)}) copy-start(u32[32]{0:T(128)} %constant.104) | copy-start | bytes 388
  9.8 13.0 %all-to-all-start = ((bf16[256,2,512]{2,0,1:T(8,128)(2,1)}), bf16[256,2,512]{2,0,1:T(8,128)(2,1)S(1)}, u32[]{:S(2)}, u32[]{:S(2)}) async-start(bf16[256,2,512]{2,0,1:T(8,128)(2,1)} %bitcast.37), calls=%async_computation | async-start | bytes 1048576 | tf_op jit(solution)/shard_map/all_to_all | solution.py:35
  14.0 86.8 %all-gather.5.cloned.1.call-start = ((), (), s32[]{:S(2)}) async-start(), calls=%async_computation.3 | async-start | bytes 2621440 | tf_op jit(solution)/shard_map/all_gather | solution.py:36
  22.8 0.8 copy-start.1
  26.2 11.0 %all-to-all-start.1 = ((bf16[4,64,256]{2,1,0:T(8,128)(2,1)}), bf16[4,64,256]{2,1,0:T(8,128)(2,1)S(1)}, u32[]{:S(2)}, u32[]{:S(2)}) async-start(bf16[4,64,256]{2,1,0:T(8,128)(2,1)} %select_select_fusion), calls=%async_computation.1 | async-start | bytes 262144 | tf_op jit(solution)/shard_map/all_to_all | solution.py:67
Sparse Core Ops, SparseCore 0:
  10.1 44.1 all-gather.2
  55.9 44.9 all-gather.4
where the time goes:
time: 144 us; the launch traced here: 143 us
  waiting for transfers between devices  47.9 us (33%)
  blocking collectives  30.3 us (21%)
  matrix products  27 us (19%)
  between operations  14.8 us (10%)
  starting transfers between devices  9.39 us (7%)
  other arithmetic  6.97 us (5%)
  local copies, waits for them, and re-layouts  6.81 us (5%)
    all_gather x1, waiting for transfers between devices, shards(): factor_cols = lax.all_gather(mixed, 'rows', axis=0, tiled=True)  36.9 us
    dot_general x8, matrix products, block_total(): projected = jnp.dot(values, factor_cols, preferred_element_type=jnp.float32)  26.1 us
    all_gather x1, blocking collectives, shards(): column_rows = lax.all_gather(piece, 'rows', axis=0, tiled=True)  13.2 us
    all_gather x1, blocking collectives, shards(): arrived = lax.all_gather(moved, ('cols', 'sub'), axis=1, tiled=True)  9.63 us
    all_to_all x1, waiting for transfers between devices, shards(): lax.all_to_all(factor, 'cols', split_axis=1, concat_axis=0, tiled=True)  5.88 us
    all_to_all x1, starting transfers between devices, shards(): lax.all_to_all(outgoing, 'rows', split_axis=0, concat_axis=0, tiled=True)  5.12 us
    unnamed x1, blocking collectives  5 us
    all_to_all x1, waiting for transfers between devices, shards(): lax.all_to_all(outgoing, 'rows', split_axis=0, concat_axis=0, tiled=True)  4.48 us
  transfers between devices with their start and end apart: 4, of which 3 were waited for; matrix products, arithmetic and copies ran while one was open for 8% of the time, Pallas kernels for 0%

commit v1 on v0

v1 whole, which is shorter than its diff:
```python
import functools
import math

import jax
import jax.numpy as jnp
from jax import lax
from jax.experimental import pallas as pl
from jax.experimental.pallas import tpu as pltpu
from jax.sharding import PartitionSpec as P

PANEL_DEV = 64
LOG2E = math.log2(math.e)
NT = (((1,), (1,)), ((), ()))


def lane_norms(block):
    sq = jnp.square(block.astype(jnp.float32))
    return lane_sums(sq)


def lane_sums(values):
    part = values[:, :128]
    for at in range(128, values.shape[1], 128):
        part = part + values[:, at:at + 128]
    return jnp.sum(part.T, axis=0, keepdims=True)


def kernel(dims, data_ref, land_ref, factor_ref, sel_ref, lev_ref, panel_ref,
           lbuf, fbuf, xbuf, dbuf, gbuf, abuf, chbuf, pbuf, tot, tbuf, cross, acc, lsq,
           lsem, fsem, xsem, dsem, asem, csem, psem, tsem, lcl, ss):
    R, C, S = dims
    NP = R // 2
    SL, D = data_ref.shape
    Lb = land_ref.shape[0]
    W = factor_ref.shape[1] // C
    SLC = SL // C
    NQ = C * S
    Qs = abuf.shape[1]
    PCD = pbuf.shape[1]
    rate = 0.3 / math.sqrt(8.0 * D)
    k = rate * LOG2E
    g = lax.axis_index("groups")
    r = lax.axis_index("rows")
    c = lax.axis_index("cols")
    s = lax.axis_index("sub")
    pair = r // 2
    par = lax.rem(r, 2)
    own = s == par
    other = s != par
    pending = []

    def send(src, dst, rsem, dev, cond=None):
        at = ss.at[len(pending)]
        copy = pltpu.make_async_remote_copy(
            src_ref=src, dst_ref=dst, send_sem=at, recv_sem=rsem,
            device_id=(g,) + tuple(dev), device_id_type=pl.DeviceIdType.MESH)
        pending.append((copy, cond))
        if cond is None:
            copy.start()
        else:
            pl.when(cond)(copy.start)

    def local(src, dst, sem, cond=None):
        copy = pltpu.make_async_copy(src, dst, sem)
        if cond is None:
            copy.start()
        else:
            pl.when(cond)(copy.start)

    def arrive(slot, sem, cond=None):
        copy = pltpu.make_async_copy(slot, slot, sem)
        if cond is None:
            copy.wait()
        else:
            pl.when(cond)(copy.wait)

    def pair_row(e, parity):
        return lax.rem(pair + e, NP) * 2 + parity

    def col_at(j):
        return lax.rem(c + j, C)

    barrier = pltpu.get_barrier_semaphore()

    def greet(i, carry):
        ri = i // NQ
        rest = lax.rem(i, NQ)
        pl.semaphore_signal(barrier, inc=1, device_id=(g, ri, rest // S, lax.rem(rest, S)),
                            device_id_type=pl.DeviceIdType.MESH)
        return carry

    lax.fori_loop(0, R * NQ, greet, 0)
    pl.semaphore_wait(barrier, R * NQ)

    mate = par + pair * 2 + 1 - 2 * par
    local(land_ref, lbuf.at[0, par, c], lcl.at[0])
    for e in range(1, NP):
        send(land_ref, lbuf.at[NP - e, s, c], lsem.at[NP - e, s, c], (pair_row(e, par), c, s), own)
    send(land_ref, lbuf.at[0, s, c], lsem.at[0, s, c], (mate, c, s), own)
    for j in range(1, C):
        send(land_ref, lbuf.at[0, s, c], lsem.at[0, s, c], (r, col_at(j), s), own)
    part = pl.ds(pl.multiple_of(c * SLC, SLC), SLC)
    send(data_ref.at[part], dbuf.at[c], dsem.at[c], (mate, c, s), own)
    for j in range(C):
        at = col_at(j)
        rows = pl.ds(pl.multiple_of(at * SLC, SLC), SLC)
        local(data_ref.at[rows], dbuf.at[at], dsem.at[at], own)
    for j in range(1, C):
        at = col_at(j)
        send(factor_ref.at[:, pl.ds(pl.multiple_of(at * W, W), W)], xbuf.at[c], xsem.at[c], (r, at, s))

    def spread(src, c0):
        for e in list(range(1, NP)) + [0]:
            slot = (NP - e) % NP
            cond = None if e else other
            send(src, fbuf.at[slot, par, c0], fsem.at[slot, par, c0], (pair_row(e, s), c, par), cond)
        local(src, fbuf.at[0, par, c0], fsem.at[0, par, c0], own)

    spread(factor_ref.at[:, pl.ds(pl.multiple_of(c * W, W), W)], c)

    per = min(R, max(1, 256 // Qs))

    def gather(i, carry):
        rows = pl.ds(pl.multiple_of(i * per * Qs, per * Qs), per * Qs)
        target = sel_ref[rows]
        lanes = lax.broadcasted_iota(jnp.int32, (per * Qs, SL), 1)
        hot = jnp.where(lanes == target, 1.0, 0.0).astype(jnp.bfloat16)
        got = jnp.dot(hot, data_ref[...], preferred_element_type=jnp.float32)
        gbuf[pl.ds(i * per, per)] = got.astype(jnp.bfloat16).reshape(per, Qs, D)
        return carry

    lax.fori_loop(0, R // per, gather, 0)
    for e in range(1, R):
        to = lax.rem(r + e, R)
        send(gbuf.at[to], abuf.at[R - e], asem.at[R - e], (to, c, s))

    arrive(lbuf.at[0, par, c], lcl.at[0])
    for d in range(NP):
        arrive(lbuf.at[d, s, c], lsem.at[d, s, c], other if d == 0 else None)
        block = lbuf.at[d, s, c]
        if d:
            send(block, block, lsem.at[d, s, c], (mate, c, s), own)
        for j in range(1, C):
            send(block, block, lsem.at[d, s, c], (r, col_at(j), s), None if d else other)
        send(block, block, lsem.at[d, s, c], (r, c, 1 - s), None if d else other)
    for d in range(NP):
        for j in range(1, C):
            at = col_at(j)
            arrive(lbuf.at[d, s, at], lsem.at[d, s, at])
            block = lbuf.at[d, s, at]
            send(block, block, lsem.at[d, s, at], (r, c, 1 - s))

    for j in range(1, C):
        at = col_at(j)
        arrive(xbuf.at[at], xsem.at[at])
        spread(xbuf.at[at], at)

    q = c * S + s
    total = gbuf[r].astype(jnp.float32)
    for e in range(1, R):
        arrive(abuf.at[R - e], asem.at[R - e])
        total = total + abuf[R - e].astype(jnp.float32)
    chbuf[q] = total.astype(jnp.bfloat16)
    for e in range(1, NQ):
        to = lax.rem(q + e, NQ)
        send(chbuf.at[q], chbuf.at[q], csem.at[q], (r, to // S, lax.rem(to, S)))

    for d in range(NP):
        for j in range(C):
            at = col_at(j)
            arrive(lbuf.at[d, 1 - s, at], lsem.at[d, 1 - s, at], own if d == 0 and j == 0 else None)
    arrive(dbuf.at[c], dsem.at[c])
    for j in range(1, C):
        send(dbuf.at[c], dbuf.at[c], dsem.at[c], (r, col_at(j), s), other)

    LM = R * C * Lb
    lands = lbuf.reshape(LM, D)
    LC = min(512, LM)
    for at in range(0, LM, LC):
        lsq[:, at:at + LC] = lane_norms(lands[at:at + LC]) * (-k)

    RB = min(256, SLC)

    def values_of(at):
        def body(i, carry):
            rows = pl.ds(pl.multiple_of(i * RB, RB), RB)
            block = dbuf[at, rows]
            up = block.astype(jnp.float32)
            bias = (2.0 * D - jnp.sum(up * up, axis=1, keepdims=True)) * k
            for lo in range(0, LM, LC):
                x = lax.dot_general(block, lands[lo:lo + LC], NT, preferred_element_type=jnp.float32)
                cross[at, rows, lo:lo + LC] = jnp.exp2(x * (2.0 * k) + (bias + lsq[:, lo:lo + LC])).astype(jnp.bfloat16)
            return carry

        lax.fori_loop(0, SLC // RB, body, 0)

    values_of(c)

    for e in range(1, NQ):
        at = lax.rem(q + e, NQ)
        arrive(chbuf.at[at], csem.at[at])
    flat = chbuf.reshape(NQ * Qs, D)
    piece = pl.ds(pl.multiple_of(c * PCD, PCD), PCD)
    for e in range(1, R):
        to = lax.rem(r + e, R)
        send(flat.at[piece], pbuf.at[r], psem.at[r], (to, c, s))
    local(flat.at[piece], pbuf.at[r], psem.at[r])

    for j in range(1, C):
        at = col_at(j)
        arrive(dbuf.at[at], dsem.at[at])
        values_of(at)

    for e in range(R):
        at = lax.rem(r + e, R)
        arrive(pbuf.at[at], psem.at[at])
    rows_in = flat[...]
    cols_in = pbuf[...].reshape(R * PCD, D)
    up = rows_in.astype(jnp.float32)
    bias = (2.0 * D - jnp.sum(up * up, axis=1, keepdims=True)) * k
    x = lax.dot_general(rows_in, cols_in, NT, preferred_element_type=jnp.float32)
    panel_ref[...] = jnp.exp2(x * (2.0 * k) + (bias - k * lane_norms(cols_in)))

    def take(d):
        for j in range(C):
            at = col_at(j)
            arrive(fbuf.at[d, s, at], fsem.at[d, s, at])
            block = fbuf.at[d, s, at]
            send(block, block, fsem.at[d, s, at], (r, c, 1 - s))
        for j in range(C):
            at = col_at(j)
            arrive(fbuf.at[d, 1 - s, at], fsem.at[d, 1 - s, at])

    KA = 2 * C * Lb
    flat_f = fbuf.reshape(LM, W)
    take(0)

    def first(i, carry):
        rows = pl.ds(pl.multiple_of(lax.rem(i, SLC // RB) * RB, RB), RB)
        at = i // (SLC // RB)
        acc[at, rows] = jnp.dot(cross[at, rows, :KA], flat_f[:KA], preferred_element_type=jnp.float32)
        return carry

    lax.fori_loop(0, SL // RB, first, 0)
    for d in range(1, NP):
        take(d)

    def last(i, carry):
        start = pl.multiple_of(lax.rem(i, SLC // RB) * RB, RB)
        rows = pl.ds(start, RB)
        at = i // (SLC // RB)
        proj = acc[at, rows]
        if NP > 1:
            proj = proj + jnp.dot(cross[at, rows, KA:], flat_f[KA:], preferred_element_type=jnp.float32)
        tot[at, :, rows] = lane_sums(proj * proj)
        return carry

    lax.fori_loop(0, SL // RB, last, 0)

    mine = par * C + c
    for j in range(C):
        at = col_at(j)
        for flip in range(2):
            core = s if flip == 0 else 1 - s
            cond = other if j == 0 and flip == 0 else None
            send(tot.at[at], tbuf.at[mine], tsem.at[mine], (pair * 2 + s, at, core), cond)
    local(tot.at[c], tbuf.at[mine], tsem.at[mine], own)
    approx = jnp.zeros((1, SLC), jnp.float32)
    for i in range(2 * C):
        arrive(tbuf.at[i], tsem.at[i])
        approx = approx + tbuf[i]
    lev_ref[...] = (math.exp(2.0 * rate * D) - approx) / 8.0
    for copy, cond in pending:
        if cond is None:
            copy.wait_send()
        else:
            pl.when(cond)(copy.wait_send)


def shards(dims, data_rows, landmarks, factor, chosen_owner, chosen_local):
    R, C, S = dims
    NP = R // 2
    SL, D = data_rows.shape
    Lb = landmarks.shape[0]
    W = factor.shape[1] // C
    NQ = C * S
    M2 = chosen_local.shape[0]
    Qs = M2 // (R * NQ)
    PCD = PANEL_DEV // C
    SLC = SL // C
    LM = R * C * Lb
    r = lax.axis_index("rows")
    q = lax.axis_index("cols") * S + lax.axis_index("sub")
    sel = jnp.where(chosen_owner[:, 0] == r, chosen_local, -1).reshape(R, NQ, Qs)
    sel = lax.dynamic_index_in_dim(sel, q, 1, keepdims=False).reshape(R * Qs, 1)
    vm = pl.BlockSpec(memory_space=pltpu.VMEM)
    bf = jnp.bfloat16
    sends = (NP - 1) + 1 + (C - 1) + 1 + (C - 1) + NP * C + (R - 1)
    sends += NP * (1 + C) + NP * (C - 1) + (NQ - 1) + (C - 1) + (R - 1) + NP * C + 2 * C
    dma = pltpu.SemaphoreType.DMA
    lev, panel = pl.pallas_call(
        functools.partial(kernel, dims),
        out_shape=(jax.ShapeDtypeStruct((1, SLC), jnp.float32),
                   jax.ShapeDtypeStruct((M2 // R, R * PCD), jnp.float32)),
        in_specs=[vm] * 4,
        out_specs=(vm, vm),
        scratch_shapes=[
            pltpu.VMEM((NP, 2, C, Lb, D), bf),
            pltpu.VMEM((NP, 2, C, Lb, W), bf),
            pltpu.VMEM((C, Lb, W), bf),
            pltpu.VMEM((C, SLC, D), bf),
            pltpu.VMEM((R, Qs, D), bf),
            pltpu.VMEM((R, Qs, D), bf),
            pltpu.VMEM((NQ, Qs, D), bf),
            pltpu.VMEM((R, PCD, D), bf),
            pltpu.VMEM((C, 1, SLC), jnp.float32),
            pltpu.VMEM((2 * C, 1, SLC), jnp.float32),
            pltpu.VMEM((C, SLC, LM), bf),
            pltpu.VMEM((C, SLC, W), jnp.float32),
            pltpu.VMEM((1, LM), jnp.float32),
            dma((NP, 2, C)), dma((NP, 2, C)), dma((C,)), dma((C,)), dma((R,)), dma((NQ,)), dma((R,)),
            dma((2 * C,)), dma((1,)), dma((sends,)),
        ],
        compiler_params=pltpu.CompilerParams(
            collective_id=0, has_side_effects=True, vmem_limit_bytes=60 * 2**20),
        name="leverage_panel",
    )(data_rows, landmarks, factor, sel)
    return lev.reshape(SLC), panel


def solution(mesh):
    placed = (
        P(("groups", "rows"), None),
        P(("groups", "rows", "cols"), None),
        P(("groups", "rows", "cols"), "sub"),
        P("groups", None),
        P("groups"),
    )
    dims = tuple(mesh.shape[name] for name in ("rows", "cols", "sub"))
    return jax.shard_map(
        functools.partial(shards, dims),
        mesh=mesh,
        in_specs=placed,
        out_specs=(P(("groups", "rows", "cols")), P(("groups", "rows"), "cols")),
        check_vma=False,
    )
```

time: 144 us -> 66.4 us (0.46)
  Pallas kernels: 0 us -> 61.1 us
  waiting for transfers between devices: 47.9 us -> 0 us
  blocking collectives: 30.3 us -> 0 us
  matrix products: 27 us -> 0 us
  between operations: 14.8 us -> 0.68 us
  starting transfers between devices: 9.39 us -> 0 us
  other arithmetic: 6.97 us -> 0.03 us
  local copies, waits for them, and re-layouts: 6.81 us -> 4.4 us
    pallas_call x0 -> x1, Pallas kernels: none -> 61.1 us  [shards(): pl.pallas_call(functools.partial(kernel, dims), out_shape=(jax.ShapeDtype...]
    all_gather x2 -> x0, waiting for transfers between devices: 36.9 us -> none  [the longest x1 36.9 us: shards(): factor_cols = lax.all_gather(mixed, 'rows', axis=0, tiled=True)]
    dot_general x9 -> x0, matrix products: 27 us -> none  [the longest x8 26.1 us: block_total(): projected = jnp.dot(values, factor_cols, preferred_element_type=jnp.float32)]
    all_gather x2 -> x0, blocking collectives: 22.9 us -> none  [the longest x1 13.2 us: shards(): column_rows = lax.all_gather(piece, 'rows', axis=0, tiled=True)]
    all_to_all x2 -> x0, waiting for transfers between devices: 10.4 us -> none  [the longest x1 5.88 us: shards(): lax.all_to_all(factor, 'cols', split_axis=1, concat_axis=0, tiled=True)]
    all_to_all x2 -> x0, starting transfers between devices: 9.35 us -> none  [the longest x1 5.12 us: shards(): lax.all_to_all(outgoing, 'rows', split_axis=0, concat_axis=0, tiled=True)]
    unnamed x1 -> x0, blocking collectives: 5 us -> none
    reduce_sum x13 -> x0, other arithmetic: 3.28 us -> none  [the longest x11 2.84 us: squared_norms(): return jnp.sum(jnp.square(rows_in.astype(jnp.float32)), axis=1)]
  transfers between devices with their start and end apart: 4 -> 0, of which waited for: 3 -> 0; matrix products, arithmetic and copies ran while one was open for 8% -> 0% of each run, Pallas kernels for 0% -> 0%
where the time goes in v1:
time: 66.4 us; the launch traced here: 66.2 us
  Pallas kernels  61.1 us (92%)
  local copies, waits for them, and re-layouts  4.4 us (7%)
  between operations  0.68 us (1%)
    pallas_call x1, Pallas kernels, shards(): pl.pallas_call(functools.partial(kernel, dims), out_shape=(jax.ShapeDtype...  61.1 us
    unnamed x8, local copies, waits for them, and re-layouts  3.5 us

profile of v1, /device:TPU:0, one launch (start us, length us, event | category | flops | bytes accessed | tf_op | source)
XLA Modules:
  0.0 66.2 jit_solution(10842534208701084110)
XLA Ops:
  0.6 0.0 copy-start
  0.6 0.0 copy-start.1
  0.7 0.7 %copy-done = s32[1024,1]{0,1:T(1,128)S(1)} copy-done((s32[1024,1]{0,1:T(1,128)S(1)}, s32[1024,1]{0,1:T(1,128)}, u32[]{:S(2)}) %copy-start) | copy-done | bytes 4120
  1.3 0.0 copy-done.1
  1.4 0.1 reshape.16
  1.5 0.8 %reshape.19.sel_ref = s32[256,1]{1,0:T(8,128)} reshape(s32[4,64]{1,0:T(4,128)S(1)} %dynamic-slice_reduce_fusion) | data formatting | bytes 2048 | tf_op jit(solution)/shard_map/reshape | solution.py:295
  2.3 61.1 %leverage_panel.1 = (f32[1,1024]{1,0:T(1,128)}, f32[256,128]{1,0:T(8,128)}) custom-call(bf16[2048,256]{1,0:T(8,128)(2,1)} %data_ref.1, bf16[256,256]{1,0:T(8,128)(2,1)} %land_ref.1, bf16[256,1024]{1,0:T(8,128)(2,1)} %factor_ref.1, s32[256,1]{1,0:T(8,128)} %reshape.19.sel_ref), custom_call_target="tpu_custom_call" | custom-call | tf_op jit(solution)/shard_map/leverage_panel/pallas_call | solution.py:301
  63.4 0.0 copy-start.2
  63.4 0.7 %copy-done.2 = f32[1,1024]{1,0:T(1,128)S(1)} copy-done((f32[1,1024]{1,0:T(1,128)S(1)}, f32[1,1024]{1,0:T(1,128)}, u32[]{:S(2)}) %copy-start.2) | copy-done | bytes 4120
  64.0 0.6 copy.10
  64.6 1.6 %copy.11 = f32[256,128]{1,0:T(8,128)} copy(f32[256,128]{1,0:T(8,128)} %get-tuple-element.9) | data formatting | bytes 262144
  (3 shorter events, 0.1 us)
Async XLA Ops:
  0.6 0.7 %copy-start = (s32[1024,1]{0,1:T(1,128)S(1)}, s32[1024,1]{0,1:T(1,128)}, u32[]{:S(2)}) copy-start(s32[1024,1]{0,1:T(1,128)} %param.8) | copy-start | bytes 12292
  0.6 0.7 %copy-start.1 = (s32[1024]{0:T(1024)S(1)}, s32[1024]{0:T(1024)}, u32[]{:S(2)}) copy-start(s32[1024]{0:T(1024)} %param.9) | copy-start | bytes 12292
  63.4 0.7 %copy-start.2 = (f32[1,1024]{1,0:T(1,128)S(1)}, f32[1,1024]{1,0:T(1,128)}, u32[]{:S(2)}) copy-start(f32[1,1024]{1,0:T(1,128)} %get-tuple-element.4) | copy-start | bytes 12292

commit v2 on v1

--- a/solution.py
+++ b/solution.py
@@ -96,27 +96,14 @@
     local(land_ref, lbuf.at[0, par, c], lcl.at[0])
     for e in range(1, NP):
         send(land_ref, lbuf.at[NP - e, s, c], lsem.at[NP - e, s, c], (pair_row(e, par), c, s), own)
-    send(land_ref, lbuf.at[0, s, c], lsem.at[0, s, c], (mate, c, s), own)
+    for e in range(1, NP):
+        send(land_ref, lbuf.at[NP - e, 1 - s, c], lsem.at[NP - e, 1 - s, c], (pair_row(e, 1 - par), c, 1 - s), other)
+    send(land_ref, lbuf.at[0, 1 - s, c], lsem.at[0, 1 - s, c], (mate, c, 1 - s), other)
     for j in range(1, C):
         send(land_ref, lbuf.at[0, s, c], lsem.at[0, s, c], (r, col_at(j), s), own)
-    part = pl.ds(pl.multiple_of(c * SLC, SLC), SLC)
-    send(data_ref.at[part], dbuf.at[c], dsem.at[c], (mate, c, s), own)
-    for j in range(C):
-        at = col_at(j)
-        rows = pl.ds(pl.multiple_of(at * SLC, SLC), SLC)
-        local(data_ref.at[rows], dbuf.at[at], dsem.at[at], own)
     for j in range(1, C):
         at = col_at(j)
         send(factor_ref.at[:, pl.ds(pl.multiple_of(at * W, W), W)], xbuf.at[c], xsem.at[c], (r, at, s))
-
-    def spread(src, c0):
-        for e in list(range(1, NP)) + [0]:
-            slot = (NP - e) % NP
-            cond = None if e else other
-            send(src, fbuf.at[slot, par, c0], fsem.at[slot, par, c0], (pair_row(e, s), c, par), cond)
-        local(src, fbuf.at[0, par, c0], fsem.at[0, par, c0], own)
-
-    spread(factor_ref.at[:, pl.ds(pl.multiple_of(c * W, W), W)], c)
 
     per = min(R, max(1, 256 // Qs))
 
@@ -134,12 +121,35 @@
         to = lax.rem(r + e, R)
         send(gbuf.at[to], abuf.at[R - e], asem.at[R - e], (to, c, s))
 
+    def spread(src, c0):
+        for e in list(range(1, NP)) + [0]:
+            slot = (NP - e) % NP
+            cond = None if e else other
+            send(src, fbuf.at[slot, par, c0], fsem.at[slot, par, c0], (pair_row(e, s), c, par), cond)
+        local(src, fbuf.at[0, par, c0], fsem.at[0, par, c0], own)
+
+    spread(factor_ref.at[:, pl.ds(pl.multiple_of(c * W, W), W)], c)
+
+    part = pl.ds(pl.multiple_of(c * SLC, SLC), SLC)
+    send(data_ref.at[part], dbuf.at[c], dsem.at[c], (mate, c, s), own)
+    for j in range(C):
+        at = col_at(j)
+        rows = pl.ds(pl.multiple_of(at * SLC, SLC), SLC)
+        local(data_ref.at[rows], dbuf.at[at], dsem.at[at], own)
+    q = c * S + s
+    total = gbuf[r].astype(jnp.float32)
+    for e in range(1, R):
+        arrive(abuf.at[R - e], asem.at[R - e])
+        total = total + abuf[R - e].astype(jnp.float32)
+    chbuf[q] = total.astype(jnp.bfloat16)
+    for e in range(1, NQ):
+        to = lax.rem(q + e, NQ)
+        send(chbuf.at[q], chbuf.at[q], csem.at[q], (r, to // S, lax.rem(to, S)))
+
     arrive(lbuf.at[0, par, c], lcl.at[0])
     for d in range(NP):
         arrive(lbuf.at[d, s, c], lsem.at[d, s, c], other if d == 0 else None)
         block = lbuf.at[d, s, c]
-        if d:
-            send(block, block, lsem.at[d, s, c], (mate, c, s), own)
         for j in range(1, C):
             send(block, block, lsem.at[d, s, c], (r, col_at(j), s), None if d else other)
         send(block, block, lsem.at[d, s, c], (r, c, 1 - s), None if d else other)
@@ -150,20 +160,20 @@
             block = lbuf.at[d, s, at]
             send(block, block, lsem.at[d, s, at], (r, c, 1 - s))
 
+    for e in range(1, NQ):
+        at = lax.rem(q + e, NQ)
+        arrive(chbuf.at[at], csem.at[at])
+    flat = chbuf.reshape(NQ * Qs, D)
+    piece = pl.ds(pl.multiple_of(c * PCD, PCD), PCD)
+    for e in range(1, R):
+        to = lax.rem(r + e, R)
+        send(flat.at[piece], pbuf.at[r], psem.at[r], (to, c, s))
+    local(flat.at[piece], pbuf.at[r], psem.at[r])
+
     for j in range(1, C):
         at = col_at(j)
         arrive(xbuf.at[at], xsem.at[at])
         spread(xbuf.at[at], at)
-
-    q = c * S + s
-    total = gbuf[r].astype(jnp.float32)
-    for e in range(1, R):
-        arrive(abuf.at[R - e], asem.at[R - e])
-        total = total + abuf[R - e].astype(jnp.float32)
-    chbuf[q] = total.astype(jnp.bfloat16)
-    for e in range(1, NQ):
-        to = lax.rem(q + e, NQ)
-        send(chbuf.at[q], chbuf.at[q], csem.at[q], (r, to // S, lax.rem(to, S)))
 
     for d in range(NP):
         for j in range(C):
@@ -196,16 +206,6 @@
 
     values_of(c)
 
-    for e in range(1, NQ):
-        at = lax.rem(q + e, NQ)
-        arrive(chbuf.at[at], csem.at[at])
-    flat = chbuf.reshape(NQ * Qs, D)
-    piece = pl.ds(pl.multiple_of(c * PCD, PCD), PCD)
-    for e in range(1, R):
-        to = lax.rem(r + e, R)
-        send(flat.at[piece], pbuf.at[r], psem.at[r], (to, c, s))
-    local(flat.at[piece], pbuf.at[r], psem.at[r])
-
     for j in range(1, C):
         at = col_at(j)
         arrive(dbuf.at[at], dsem.at[at])
@@ -219,7 +219,7 @@
     up = rows_in.astype(jnp.float32)
     bias = (2.0 * D - jnp.sum(up * up, axis=1, keepdims=True)) * k
     x = lax.dot_general(rows_in, cols_in, NT, preferred_element_type=jnp.float32)
-    panel_ref[...] = jnp.exp2(x * (2.0 * k) + (bias - k * lane_norms(cols_in)))
+    panel_ref[...] = x * (2.0 * k) + (bias - k * lane_norms(cols_in))
 
     def take(d):
         for j in range(C):
@@ -269,7 +269,7 @@
     for i in range(2 * C):
         arrive(tbuf.at[i], tsem.at[i])
         approx = approx + tbuf[i]
-    lev_ref[...] = (math.exp(2.0 * rate * D) - approx) / 8.0
+    lev_ref[...] = approx
     for copy, cond in pending:
         if cond is None:
             copy.wait_send()
@@ -319,13 +319,14 @@
             pltpu.VMEM((C, SLC, W), jnp.float32),
             pltpu.VMEM((1, LM), jnp.float32),
             dma((NP, 2, C)), dma((NP, 2, C)), dma((C,)), dma((C,)), dma((R,)), dma((NQ,)), dma((R,)),
-            dma((2 * C,)), dma((1,)), dma((sends,)),
+            dma((2 * C,)), dma((1,)), dma((sends + 8,)),
         ],
         compiler_params=pltpu.CompilerParams(
             collective_id=0, has_side_effects=True, vmem_limit_bytes=60 * 2**20),
         name="leverage_panel",
     )(data_rows, landmarks, factor, sel)
-    return lev.reshape(SLC), panel
+    rate = 0.3 / math.sqrt(8.0 * D)
+    return (math.exp(2.0 * rate * D) - lev.reshape(SLC)) / 8.0, jnp.exp2(panel)
 
 
 def solution(mesh):

time: 66.4 us -> 61.5 us (0.926)
  Pallas kernels: 61.1 us -> 56.1 us
  other arithmetic: 0.03 us -> 2.88 us
  local copies, waits for them, and re-layouts: 4.4 us -> 1.57 us
    pallas_call x1, Pallas kernels: 61.1 us -> 56.1 us  [shards(): pl.pallas_call(functools.partial(kernel, dims), out_shape=(jax.ShapeDtype...]
    unnamed x8 -> x4, local copies, waits for them, and re-layouts: 3.5 us -> 0.67 us
    exp2 x0 -> x1, other arithmetic: none -> 1.58 us  [shards(): jnp.exp2(panel)]
    div x0 -> x1, other arithmetic: none -> 1.27 us  [shards(): (math.exp(2.0 * rate * D) - lev.reshape(SLC)) / 8.0]
where the time goes in v2:
time: 61.5 us; the launch traced here: 61.3 us
  Pallas kernels  56.1 us (91%)
  other arithmetic  2.88 us (5%)
  local copies, waits for them, and re-layouts  1.57 us (3%)
  between operations  0.68 us (1%)
    pallas_call x1, Pallas kernels, shards(): pl.pallas_call(functools.partial(kernel, dims), out_shape=(jax.ShapeDtype...  56.1 us
    exp2 x1, other arithmetic, shards(): jnp.exp2(panel)  1.58 us
    div x1, other arithmetic, shards(): (math.exp(2.0 * rate * D) - lev.reshape(SLC)) / 8.0  1.27 us

profile of v2, /device:TPU:0, one launch (start us, length us, event | category | flops | bytes accessed | tf_op | source)
XLA Modules:
  0.0 61.3 jit_solution(9371257188603318703)
XLA Ops:
  0.6 0.0 copy-start
  0.6 0.0 copy-start.1
  0.7 0.7 %copy-done = s32[1024,1]{0,1:T(1,128)S(1)} copy-done((s32[1024,1]{0,1:T(1,128)S(1)}, s32[1024,1]{0,1:T(1,128)}, u32[]{:S(2)}) %copy-start) | copy-done | bytes 4120
  1.3 0.0 copy-done.1
  1.4 0.1 reshape.18
  1.5 0.8 %reshape.20.sel_ref = s32[256,1]{1,0:T(8,128)} reshape(s32[4,64]{1,0:T(4,128)S(1)} %dynamic-slice_reduce_fusion) | data formatting | bytes 2048 | tf_op jit(solution)/shard_map/reshape | solution.py:295
  2.3 56.1 %leverage_panel.1 = (f32[1,1024]{1,0:T(1,128)}, f32[256,128]{1,0:T(8,128)}) custom-call(bf16[2048,256]{1,0:T(8,128)(2,1)} %data_ref.1, bf16[256,256]{1,0:T(8,128)(2,1)} %land_ref.1, bf16[256,1024]{1,0:T(8,128)(2,1)} %factor_ref.1, s32[256,1]{1,0:T(8,128)} %reshape.20.sel_ref), custom_call_target="tpu_custom_call" | custom-call | tf_op jit(solution)/shard_map/leverage_panel/pallas_call | solution.py:301
  58.4 1.3 %subtract_multiply_fusion = f32[1,1024]{1,0:T(1,128)} fusion(f32[1,1024]{1,0:T(1,128)} %get-tuple-element.4), kind=kLoop, calls=%fused_computation.2 | loop fusion | flops 2048 | bytes 8192 | tf_op jit(solution)/shard_map/div | solution.py:329
  59.7 1.6 %multiply_exponential_fusion = f32[256,128]{1,0:T(8,128)} fusion(f32[256,128]{1,0:T(8,128)} %get-tuple-element.5), kind=kLoop, calls=%fused_computation | loop fusion | flops 32768 | bytes 262144 | tf_op jit(solution)/shard_map/exp2 | solution.py:329
  (3 shorter events, 0.1 us)
Async XLA Ops:
  0.6 0.7 %copy-start = (s32[1024,1]{0,1:T(1,128)S(1)}, s32[1024,1]{0,1:T(1,128)}, u32[]{:S(2)}) copy-start(s32[1024,1]{0,1:T(1,128)} %param.8) | copy-start | bytes 12292
  0.6 0.7 %copy-start.1 = (s32[1024]{0:T(1024)S(1)}, s32[1024]{0:T(1024)}, u32[]{:S(2)}) copy-start(s32[1024]{0:T(1024)} %param.9) | copy-start | bytes 12292

commit v3 on v2

--- a/solution.py
+++ b/solution.py
@@ -189,7 +189,7 @@
     for at in range(0, LM, LC):
         lsq[:, at:at + LC] = lane_norms(lands[at:at + LC]) * (-k)
 
-    RB = min(256, SLC)
+    RB = min(1024, SLC)
 
     def values_of(at):
         def body(i, carry):
@@ -211,6 +211,27 @@
         arrive(dbuf.at[at], dsem.at[at])
         values_of(at)
 
+    def take(d):
+        for j in range(C):
+            at = col_at(j)
+            arrive(fbuf.at[d, s, at], fsem.at[d, s, at])
+            block = fbuf.at[d, s, at]
+            send(block, block, fsem.at[d, s, at], (r, c, 1 - s))
+        for j in range(C):
+            at = col_at(j)
+            arrive(fbuf.at[d, 1 - s, at], fsem.at[d, 1 - s, at])
+
+    KA = 2 * C * Lb
+    flat_f = fbuf.reshape(LM, W)
+    take(0)
+
+    def first(i, carry):
+        rows = pl.ds(pl.multiple_of(lax.rem(i, SLC // RB) * RB, RB), RB)
+        at = i // (SLC // RB)
+        acc[at, rows] = jnp.dot(cross[at, rows, :KA], flat_f[:KA], preferred_element_type=jnp.float32)
+        return carry
+
+    lax.fori_loop(0, SL // RB, first, 0)
     for e in range(R):
         at = lax.rem(r + e, R)
         arrive(pbuf.at[at], psem.at[at])
@@ -221,27 +242,6 @@
     x = lax.dot_general(rows_in, cols_in, NT, preferred_element_type=jnp.float32)
     panel_ref[...] = x * (2.0 * k) + (bias - k * lane_norms(cols_in))
 
-    def take(d):
-        for j in range(C):
-            at = col_at(j)
-            arrive(fbuf.at[d, s, at], fsem.at[d, s, at])
-            block = fbuf.at[d, s, at]
-            send(block, block, fsem.at[d, s, at], (r, c, 1 - s))
-        for j in range(C):
-            at = col_at(j)
-            arrive(fbuf.at[d, 1 - s, at], fsem.at[d, 1 - s, at])
-
-    KA = 2 * C * Lb
-    flat_f = fbuf.reshape(LM, W)
-    take(0)
-
-    def first(i, carry):
-        rows = pl.ds(pl.multiple_of(lax.rem(i, SLC // RB) * RB, RB), RB)
-        at = i // (SLC // RB)
-        acc[at, rows] = jnp.dot(cross[at, rows, :KA], flat_f[:KA], preferred_element_type=jnp.float32)
-        return carry
-
-    lax.fori_loop(0, SL // RB, first, 0)
     for d in range(1, NP):
         take(d)
 

time: 61.5 us -> 58.7 us (0.954)
  Pallas kernels: 56.1 us -> 53.3 us
    pallas_call x1, Pallas kernels: 56.1 us -> 53.3 us  [shards(): pl.pallas_call(functools.partial(kernel, dims), out_shape=(jax.ShapeDtype...]
where the time goes in v3:
time: 58.7 us; the launch traced here: 58.4 us
  Pallas kernels  53.3 us (91%)
  other arithmetic  2.88 us (5%)
  local copies, waits for them, and re-layouts  1.57 us (3%)
  between operations  0.68 us (1%)
    pallas_call x1, Pallas kernels, shards(): pl.pallas_call(functools.partial(kernel, dims), out_shape=(jax.ShapeDtype...  53.3 us
    exp2 x1, other arithmetic, shards(): jnp.exp2(panel)  1.58 us
    div x1, other arithmetic, shards(): (math.exp(2.0 * rate * D) - lev.reshape(SLC)) / 8.0  1.27 us

profile of v3, /device:TPU:0, one launch (start us, length us, event | category | flops | bytes accessed | tf_op | source)
XLA Modules:
  0.0 58.4 jit_solution(8809873345337376393)
XLA Ops:
  0.6 0.0 copy-start
  0.6 0.0 copy-start.1
  0.7 0.7 %copy-done = s32[1024,1]{0,1:T(1,128)S(1)} copy-done((s32[1024,1]{0,1:T(1,128)S(1)}, s32[1024,1]{0,1:T(1,128)}, u32[]{:S(2)}) %copy-start) | copy-done | bytes 4120
  1.3 0.0 copy-done.1
  1.4 0.1 reshape.18
  1.5 0.8 %reshape.20.sel_ref = s32[256,1]{1,0:T(8,128)} reshape(s32[4,64]{1,0:T(4,128)S(1)} %dynamic-slice_reduce_fusion) | data formatting | bytes 2048 | tf_op jit(solution)/shard_map/reshape | solution.py:295
  2.3 53.3 %leverage_panel.1 = (f32[1,1024]{1,0:T(1,128)}, f32[256,128]{1,0:T(8,128)}) custom-call(bf16[2048,256]{1,0:T(8,128)(2,1)} %data_ref.1, bf16[256,256]{1,0:T(8,128)(2,1)} %land_ref.1, bf16[256,1024]{1,0:T(8,128)(2,1)} %factor_ref.1, s32[256,1]{1,0:T(8,128)} %reshape.20.sel_ref), custom_call_target="tpu_custom_call" | custom-call | tf_op jit(solution)/shard_map/leverage_panel/pallas_call | solution.py:301
  55.6 1.3 %subtract_multiply_fusion = f32[1,1024]{1,0:T(1,128)} fusion(f32[1,1024]{1,0:T(1,128)} %get-tuple-element.4), kind=kLoop, calls=%fused_computation.2 | loop fusion | flops 2048 | bytes 8192 | tf_op jit(solution)/shard_map/div | solution.py:329
  56.8 1.6 %multiply_exponential_fusion = f32[256,128]{1,0:T(8,128)} fusion(f32[256,128]{1,0:T(8,128)} %get-tuple-element.5), kind=kLoop, calls=%fused_computation | loop fusion | flops 32768 | bytes 262144 | tf_op jit(solution)/shard_map/exp2 | solution.py:329
  (3 shorter events, 0.1 us)
Async XLA Ops:
  0.6 0.7 %copy-start = (s32[1024,1]{0,1:T(1,128)S(1)}, s32[1024,1]{0,1:T(1,128)}, u32[]{:S(2)}) copy-start(s32[1024,1]{0,1:T(1,128)} %param.8) | copy-start | bytes 12292
  0.6 0.7 %copy-start.1 = (s32[1024]{0:T(1024)S(1)}, s32[1024]{0:T(1024)}, u32[]{:S(2)}) copy-start(s32[1024]{0:T(1024)} %param.9) | copy-start | bytes 12292

commit v4 on v3

--- a/solution.py
+++ b/solution.py
@@ -231,7 +231,26 @@
         acc[at, rows] = jnp.dot(cross[at, rows, :KA], flat_f[:KA], preferred_element_type=jnp.float32)
         return carry
 
-    lax.fori_loop(0, SL // RB, first, 0)
+    for d in range(1, NP):
+        take(d)
+    def last(i, carry):
+        start = pl.multiple_of(lax.rem(i, SLC // RB) * RB, RB)
+        rows = pl.ds(start, RB)
+        at = i // (SLC // RB)
+        proj = jnp.dot(cross[at, rows], flat_f[...], preferred_element_type=jnp.float32)
+        tot[at, :, rows] = lane_sums(proj * proj)
+        return carry
+
+    lax.fori_loop(0, SL // RB, last, 0)
+
+    mine = par * C + c
+    for j in range(C):
+        at = col_at(j)
+        for flip in range(2):
+            core = s if flip == 0 else 1 - s
+            cond = other if j == 0 and flip == 0 else None
+            send(tot.at[at], tbuf.at[mine], tsem.at[mine], (pair * 2 + s, at, core), cond)
+    local(tot.at[c], tbuf.at[mine], tsem.at[mine], own)
     for e in range(R):
         at = lax.rem(r + e, R)
         arrive(pbuf.at[at], psem.at[at])
@@ -242,29 +261,7 @@
     x = lax.dot_general(rows_in, cols_in, NT, preferred_element_type=jnp.float32)
     panel_ref[...] = x * (2.0 * k) + (bias - k * lane_norms(cols_in))
 
-    for d in range(1, NP):
-        take(d)
-
-    def last(i, carry):
-        start = pl.multiple_of(lax.rem(i, SLC // RB) * RB, RB)
-        rows = pl.ds(start, RB)
-        at = i // (SLC // RB)
-        proj = acc[at, rows]
-        if NP > 1:
-            proj = proj + jnp.dot(cross[at, rows, KA:], flat_f[KA:], preferred_element_type=jnp.float32)
-        tot[at, :, rows] = lane_sums(proj * proj)
-        return carry
-
-    lax.fori_loop(0, SL // RB, last, 0)
-
-    mine = par * C + c
-    for j in range(C):
-        at = col_at(j)
-        for flip in range(2):
-            core = s if flip == 0 else 1 - s
-            cond = other if j == 0 and flip == 0 else None
-            send(tot.at[at], tbuf.at[mine], tsem.at[mine], (pair * 2 + s, at, core), cond)
-    local(tot.at[c], tbuf.at[mine], tsem.at[mine], own)
+
     approx = jnp.zeros((1, SLC), jnp.float32)
     for i in range(2 * C):
         arrive(tbuf.at[i], tsem.at[i])

time: 58.7 us -> 58.1 us (0.990)
  Pallas kernels: 53.3 us -> 52.7 us
where the time goes in v4:
time: 58.1 us; the launch traced here: 57.9 us
  Pallas kernels  52.7 us (91%)
  other arithmetic  2.88 us (5%)
  local copies, waits for them, and re-layouts  1.57 us (3%)
  between operations  0.68 us (1%)
    pallas_call x1, Pallas kernels, shards(): pl.pallas_call(functools.partial(kernel, dims), out_shape=(jax.ShapeDtype...  52.7 us
    exp2 x1, other arithmetic, shards(): jnp.exp2(panel)  1.58 us
    div x1, other arithmetic, shards(): (math.exp(2.0 * rate * D) - lev.reshape(SLC)) / 8.0  1.27 us

profile of v4, /device:TPU:0, one launch (start us, length us, event | category | flops | bytes accessed | tf_op | source)
XLA Modules:
  0.0 57.9 jit_solution(9193412157334964914)
XLA Ops:
  0.6 0.0 copy-start
  0.6 0.0 copy-start.1
  0.7 0.7 %copy-done = s32[1024,1]{0,1:T(1,128)S(1)} copy-done((s32[1024,1]{0,1:T(1,128)S(1)}, s32[1024,1]{0,1:T(1,128)}, u32[]{:S(2)}) %copy-start) | copy-done | bytes 4120
  1.3 0.0 copy-done.1
  1.4 0.1 reshape.18
  1.5 0.8 %reshape.20.sel_ref = s32[256,1]{1,0:T(8,128)} reshape(s32[4,64]{1,0:T(4,128)S(1)} %dynamic-slice_reduce_fusion) | data formatting | bytes 2048 | tf_op jit(solution)/shard_map/reshape | solution.py:292
  2.3 52.7 %leverage_panel.1 = (f32[1,1024]{1,0:T(1,128)}, f32[256,128]{1,0:T(8,128)}) custom-call(bf16[2048,256]{1,0:T(8,128)(2,1)} %data_ref.1, bf16[256,256]{1,0:T(8,128)(2,1)} %land_ref.1, bf16[256,1024]{1,0:T(8,128)(2,1)} %factor_ref.1, s32[256,1]{1,0:T(8,128)} %reshape.20.sel_ref), custom_call_target="tpu_custom_call" | custom-call | tf_op jit(solution)/shard_map/leverage_panel/pallas_call | solution.py:298
  55.0 1.3 %subtract_multiply_fusion = f32[1,1024]{1,0:T(1,128)} fusion(f32[1,1024]{1,0:T(1,128)} %get-tuple-element.4), kind=kLoop, calls=%fused_computation.2 | loop fusion | flops 2048 | bytes 8192 | tf_op jit(solution)/shard_map/div | solution.py:326
  56.3 1.6 %multiply_exponential_fusion = f32[256,128]{1,0:T(8,128)} fusion(f32[256,128]{1,0:T(8,128)} %get-tuple-element.5), kind=kLoop, calls=%fused_computation | loop fusion | flops 32768 | bytes 262144 | tf_op jit(solution)/shard_map/exp2 | solution.py:326
  (3 shorter events, 0.1 us)
Async XLA Ops:
  0.6 0.7 %copy-start = (s32[1024,1]{0,1:T(1,128)S(1)}, s32[1024,1]{0,1:T(1,128)}, u32[]{:S(2)}) copy-start(s32[1024,1]{0,1:T(1,128)} %param.8) | copy-start | bytes 12292
  0.6 0.7 %copy-start.1 = (s32[1024]{0:T(1024)S(1)}, s32[1024]{0:T(1024)}, u32[]{:S(2)}) copy-start(s32[1024]{0:T(1024)} %param.9) | copy-start | bytes 12292
